TPU v7x, 256 devices: a whole 4x4x8 slice. The times are simulated.
256 devices in a mesh: seq: 64 (over y, z, core), head: 4 (over x).
Axes of the slice: x: 4, y: 4, z: 8, core: 2. Of those that a mesh axis runs over, the one named last changes fastest.
Arguments:
- inner_input: bfloat16 [16384, 8192], P('seq', 'head'), may hold values from -6 to 6
- state_input: bfloat16 [16384, 2, 1024], P('seq', None, 'head'), may hold values from -3 to 3
- gate_input: bfloat16 [16384, 8192], P('seq', 'head'), may hold values from -6 to 6
- step_input: float32 [128, 16384], P('head', 'seq'), may hold values from -4.7 to 0.6
- decay_exponent: float32 [128], P('head')
- skip_gain: float32 [128], P('head'), may hold values from 0.5 to 1.5
- documents: int32 [16384], P('seq'), may hold values from 0 to 15, never falling along the last dimension, each value on 1 to 1536 neighbouring positions
- filter_inner: float32 [4, 8192], P(None, 'head'), may hold values from -3 to 3
- filter_state: float32 [4, 2, 1024], P(None, None, 'head'), may hold values from -3 to 3
- norm_gain: float32 [8192], P('head'), may hold values from 0.1 to 1.9
- output_weight: bfloat16 [8192, 4096], P('head', 'seq'), may hold values from -0.0625 to 0.0625
Outputs:
- mixed: bfloat16 [16384, 4096], P('seq', 'head')
Inputs may be any that keep to these rules, and one draw needn't show every extreme that they name: `documents`: document numbers never fall along the sequence.
All inputs are finite; a program needn't handle non-finite values.
Results may differ from a plain program's by a relative error of at most 0.0058.
Values may be sent and summed in bfloat16 or wider, within the bound.
No kernel may reach another device: no remote copies, remote signals or barrier semaphores. Data moves between devices by JAX's collectives and lax.ppermute only.
A program may use at most 192 MiB of HBM per device.

v0:
```python
import jax
import jax.numpy as jnp
from jax import lax
from jax.sharding import PartitionSpec as P

HEAD_DIM = 64
STATE = 128
GROUPS = 8
INNER = 8192
KERNEL = 4


highest = lax.Precision.HIGHEST


def entering(part, axis, combine, identity):
    place = lax.axis_index(axis)
    gathered = jax.tree.map(lambda a: lax.all_gather(a, axis), part)
    state = jax.tree.map(lambda a, e: jnp.zeros_like(a) + jnp.asarray(e, a.dtype), part, identity)

    def one(step, state):
        return combine(
            state, jax.tree.map(lambda a: lax.dynamic_index_in_dim(a, step, 0, False), gathered)
        )

    return lax.fori_loop(0, place, one, state)


def passed_along(value, axis, steps):
    count = lax.axis_size(axis)
    initial, last = (max(0, -steps), min(count, count - steps))
    return lax.ppermute(value, axis, [(source, source + steps) for source in range(initial, last)])


def causal_conv(extended, weights, segments_wide, segment_block):
    length = segment_block.shape[0]
    running = jnp.zeros(extended[:length].shape, jnp.float32)
    for offset in range(KERNEL):
        window = extended[offset : offset + length].astype(jnp.float32)
        matches = segments_wide[offset : offset + length] == segment_block
        matches = matches.reshape((length,) + (1,) * (extended.ndim - 1))
        running = running + jnp.where(matches, window * weights[offset], jnp.float32(0.0))
    return jax.nn.silu(running).astype(jnp.bfloat16)


def span_parts(values, write_rows, read_rows, step_size, decay_rate, segment_block, prior_segment):
    length = segment_block.shape[0]
    repeat = decay_rate.shape[0] // write_rows.shape[1]
    cumulative = jnp.cumsum(decay_rate, axis=1)
    places = jnp.arange(length)
    linked = (segment_block[:, None] == segment_block[None, :]) & (
        places[:, None] >= places[None, :]
    )
    spread = cumulative[:, :, None] - cumulative[:, None, :]
    decays = jnp.exp(jnp.where(linked[None], spread, -jnp.inf))
    scores = jnp.einsum("ign,jgn->gij", read_rows, write_rows, preferred_element_type=jnp.float32)
    scores = jnp.repeat(scores, repeat, axis=0)
    mixing = (decays * scores * step_size[:, None, :]).astype(jnp.bfloat16)
    within = jnp.einsum("hij,jhp->ihp", mixing, values, preferred_element_type=jnp.float32)
    inflow = jnp.exp(cumulative) * (segment_block == prior_segment)[None, :].astype(jnp.float32)
    final_segment = segment_block[-1]
    closing = (
        jnp.exp(cumulative[:, -1:] - cumulative)
        * (segment_block == final_segment)[None, :].astype(jnp.float32)
        * step_size
    )
    weighted = (values.astype(jnp.float32) * closing.T[:, :, None]).astype(jnp.bfloat16)
    writes = jnp.repeat(write_rows, repeat, axis=1)
    deposit = jnp.einsum("jhp,jhn->hpn", weighted, writes, preferred_element_type=jnp.float32)
    fading = jnp.exp(cumulative[:, -1]) * (final_segment == prior_segment).astype(jnp.float32)
    return (within, inflow, fading, deposit)


def reading(read_rows, held_state, repeat):
    readers = jnp.repeat(read_rows, repeat, axis=1).astype(jnp.float32)
    return jnp.einsum("ihn,hpn->ihp", readers, held_state, precision=highest)


def gated_norm(outputs, gates, norm_scale):
    height = outputs.shape[0]
    gated = outputs * jax.nn.silu(gates.astype(jnp.float32))
    grouped = gated.reshape(height, -1, INNER // GROUPS)
    mean_square = jnp.mean(grouped * grouped, axis=-1, keepdims=True)
    normed = (grouped * lax.rsqrt(mean_square + 1e-05)).reshape(height, -1) * norm_scale
    return normed.astype(jnp.bfloat16)


def chain_states(through, local_state):

    def combine_pair(earlier, later):
        return (earlier[0] * later[0], later[0][:, None, None] * earlier[1] + later[1])

    neutral = (jnp.ones_like(through), jnp.zeros_like(local_state))
    return entering((through, local_state), "seq", combine_pair, neutral)[1]


def on_device(
    inner_input,
    state_input,
    gate_input,
    step_input,
    decay_exponent,
    skip_gain,
    documents,
    filter_inner,
    filter_state,
    norm_gain,
    output_weight,
):
    margin = KERNEL - 1
    length = documents.shape[0]
    head_count = decay_exponent.shape[0]
    groups = state_input.shape[2] // STATE
    repeat = head_count // groups
    before_inner, before_state, before_segments = passed_along(
        (inner_input[-margin:], state_input[-margin:], documents[-margin:].astype(jnp.bfloat16)),
        "seq",
        1,
    )
    segments_wide = jnp.concatenate([before_segments.astype(jnp.int32), documents])
    inner_conv = causal_conv(
        jnp.concatenate([before_inner, inner_input]), filter_inner, segments_wide, documents
    )
    state_conv = causal_conv(
        jnp.concatenate([before_state, state_input]), filter_state, segments_wide, documents
    )
    values = inner_conv.reshape(length, head_count, HEAD_DIM)
    write_rows = state_conv[:, 0].reshape(length, groups, STATE)
    read_rows = state_conv[:, 1].reshape(length, groups, STATE)
    step_size = jax.nn.softplus(step_input)
    decay_rate = -step_size * jnp.exp(decay_exponent)[:, None]
    skipped = skip_gain[None, :, None] * values.astype(jnp.float32)
    prior_segment = segments_wide[margin - 1]
    pieces = [
        span_parts(values, write_rows, read_rows, step_size, decay_rate, documents, prior_segment)
    ]
    local_state = jnp.zeros((head_count, HEAD_DIM, STATE), jnp.float32)
    through = jnp.ones((head_count,), jnp.float32)
    block_index = 0
    within, inflow, fading, deposit = pieces[block_index]
    local_state = fading[:, None, None] * local_state + deposit
    through = through * fading
    carried = chain_states(through, local_state)
    block_index = 0
    within, inflow, fading, deposit = pieces[block_index]
    outputs = within + inflow.T[:, :, None] * reading(read_rows, carried, repeat) + skipped
    scan_out = outputs.reshape(length, head_count * HEAD_DIM)
    normed = gated_norm(scan_out, gate_input, norm_gain)
    partial_value = jnp.dot(
        normed,
        lax.all_gather(output_weight, "seq", axis=1, tiled=True),
        preferred_element_type=jnp.float32,
    )
    return lax.psum_scatter(partial_value, "head", scatter_dimension=1, tiled=True).astype(
        jnp.bfloat16
    )


def solution(mesh):
    placed = (
        P("seq", "head"),
        P("seq", None, "head"),
        P("seq", "head"),
        P("head", "seq"),
        P("head"),
        P("head"),
        P("seq"),
        P(None, "head"),
        P(None, None, "head"),
        P("head"),
        P("head", "seq"),
    )
    return jax.shard_map(
        on_device, mesh=mesh, in_specs=placed, out_specs=P("seq", "head"), check_vma=False
    )
```

profile of v0, /device:TPU:1, one launch (start us, length us, event | category | flops | bytes accessed | tf_op | source)
XLA Modules:
  0.0 456.1 jit_solution(4651775314428934321)
XLA Ops:
  6.5 0.8 convert.3
  7.4 4.9 %collective-permute-start = (bf16[3]{0:T(256)(128)(2,1)S(1)}, bf16[3]{0:T(256)(128)(2,1)S(1)}, u32[]{:S(2)}, u32[]{:S(2)}) collective-permute-start(bf16[3]{0:T(256)(128)(2,1)S(1)} %slice.86), channel_id=1, source_target_pairs={{0,4},{4,8},{8,12},{12,16},{16,20},{20,24},{24,28},{28,32},{32,36}... | collective-permute-start | bytes 26 | tf_op jit(solution)/shard_map/ppermute | solution.py:32
  13.2 1.9 collective-permute-start.2
  15.1 0.8 slice.88
  15.9 3.9 collective-permute-start.1
  19.8 1.3 slice.112
  21.2 1.1 copy.53
  22.3 0.7 slice_bitcast_fusion.3
  23.7 0.8 copy_bitcast_fusion.1
  25.3 1.0 fusion.21
  26.9 0.8 pad_add_fusion
  28.9 2.0 slice_compare_fusion.2
  31.2 0.9 multiply_bitcast_fusion.1
  33.0 2.1 multiply_convert_fusion.1
  36.1 1.5 convolution_add_fusion
  40.1 131.3 %all-reduce = f32[2048]{0:T(1024)S(1)} all-reduce(f32[2048]{0:T(1024)S(1)} %dynamic-update-slice), channel_id=2, replica_groups=mesh['seq'=64,'head'=4] {'seq'}, use_global_device_ids=true, to_apply=%add | all-reduce | flops 2048 | bytes 16384
  171.9 2.3 fusion.1
  174.2 2.7 fusion.23
  176.9 99.1 %all-gather.7.cloned.1.call-done = f32[2048,64,128]{2,1,0:T(8,128)} async-done(((f32[32,64,128]{2,1,0:T(8,128)}), f32[2048,64,128]{2,1,0:T(8,128)}) %all-gather.7.cloned.1.call-update) | async-done | bytes 67108880 | tf_op jit(solution)/shard_map/all_gather | solution.py:18
  276.2 1.7 while.12
  276.2 1.4 bitcast_add_fusion.2
  278.3 1.1 copy-done
  279.4 3.8 fusion.3
  283.2 2.0 copy.59
  285.2 1.9 fusion.19
  287.1 4.0 mul.281
  291.2 2.2 reduce_sum.9
  294.0 2.2 copy.66
  296.2 78.8 %all-gather.5.cloned.1.call-done = bf16[2048,4096]{0,1:T(8,128)(2,1)} async-done(((bf16[2048,64]{0,1:T(8,128)(2,1)}), bf16[2048,4096]{0,1:T(8,128)(2,1)}) %all-gather.5.cloned.1.call-update) | async-done | bytes 16777232 | tf_op jit(solution)/shard_map/all_gather | solution.py:151
  375.1 13.1 %fusion.11 = f32[256,4096]{1,0:T(8,128)} fusion(bf16[2048,4096]{0,1:T(8,128)(2,1)} %all-gather.5.cloned.1.call-done, f32[256,2048]{1,0:T(8,128)} %bitcast.80, f32[2048]{0:T(1024)S(1)} %copy-done.5, f32[256,2048]{1,0:T(8,128)S(1)} %copy.59, bf16[256,2048]{1,0:T(8,128)(2,1)S(1)} %copy-done.2), kind=kOutput, calls=%fused_computation.24 | convolution fusion | flops 4299685888 | bytes 26222592 | tf_op jit(solution)/shard_map/dot_general | solution.py:149
  388.2 59.2 %reduce-scatter.2.cloned.1.call-done = f32[256,1024]{1,0:T(8,128)} async-done(((f32[256,4096]{1,0:T(8,128)}), f32[256,1024]{1,0:T(8,128)}) %reduce-scatter.2.cloned.1.call-update) | async-done | bytes 1048592 | tf_op jit(solution)/shard_map/reduce_scatter | solution.py:154
  447.4 2.1 convert_element_type.84
  (52 shorter events, 8.6 us)
Async XLA Ops:
  6.5 26.4 %copy-start.1 = (bf16[256,2048]{1,0:T(8,128)(2,1)S(1)}, bf16[256,2048]{1,0:T(8,128)(2,1)}, u32[]{:S(2)}) copy-start(bf16[256,2048]{1,0:T(8,128)(2,1)} %param.13) | copy-start | bytes 3145732
  6.5 269.5 %all-gather.7.cloned.1.call-start = ((), (), s32[]{:S(2)}) async-start(), calls=%async_computation.3 | async-start | bytes 68157440 | tf_op jit(solution)/shard_map/all_gather | solution.py:18
  7.4 18.9 %collective-permute-start = (bf16[3]{0:T(256)(128)(2,1)S(1)}, bf16[3]{0:T(256)(128)(2,1)S(1)}, u32[]{:S(2)}, u32[]{:S(2)}) collective-permute-start(bf16[3]{0:T(256)(128)(2,1)S(1)} %slice.86), channel_id=1, source_target_pairs={{0,4},{4,8},{8,12},{12,16},{16,20},{20,24},{24,28},{28,32},{32,36}... | collective-permute-start | bytes 26 | tf_op jit(solution)/shard_map/ppermute | solution.py:32
  13.2 18.9 %collective-permute-start.2 = (bf16[3,2,256]{0,2,1:T(8,128)(2,1)S(1)}, bf16[3,2,256]{0,2,1:T(8,128)(2,1)S(1)}, u32[]{:S(2)}, u32[]{:S(2)}) collective-permute-start(bf16[3,2,256]{0,2,1:T(8,128)(2,1)S(1)} %copy.52), channel_id=1, source_target_pairs={{0,4},{4,8},{8,12},{12,16},{16,20},{20,24},{24,28},{28,32},{32,36}... | collective-permute-start | bytes 9224 | tf_op jit(solution)/shard_map/ppermute | solution.py:32
  15.9 17.1 %collective-permute-start.1 = (bf16[3,2048]{1,0:T(4,128)(2,1)S(1)}, bf16[3,2048]{1,0:T(4,128)(2,1)S(1)}, u32[]{:S(2)}, u32[]{:S(2)}) collective-permute-start(bf16[3,2048]{1,0:T(4,128)(2,1)S(1)} %slice.88), channel_id=1, source_target_pairs={{0,4},{4,8},{8,12},{12,16},{16,20},{20,24},{24,28},{28,32},{32,36}... | collective-permute-start | bytes 36872 | tf_op jit(solution)/shard_map/ppermute | solution.py:32
  36.1 2.4 copy-start.6
  36.1 3.6 copy-start.3
  37.7 337.4 %all-gather.5.cloned.1.call-start = ((), (), s32[]{:S(2)}) async-start(), calls=%async_computation.1 | async-start | bytes 17039360 | tf_op jit(solution)/shard_map/all_gather | solution.py:151
  38.4 409.0 %reduce-scatter.2.cloned.1.call-start = ((), (), s32[]{:S(2)}) async-start(), calls=%async_computation.2 | async-start | bytes 5242880 | tf_op jit(solution)/shard_map/reduce_scatter | solution.py:154
  277.8 1.6 copy-start
  277.9 1.6 copy-start.4
  283.2 2.0 copy-start.2
  294.0 81.0 %copy-start.5 = (f32[2048]{0:T(1024)S(1)}, f32[2048]{0:T(1024)}, u32[]{:S(2)}) copy-start(f32[2048]{0:T(1024)} %param.22) | copy-start | bytes 24580
Sparse Core Ops, SparseCore 0:
  37.8 238.1 all-gather.6
  278.8 96.2 all-gather.4
  388.4 59.0 reduce-scatter.1
where the time goes:
time: 459 us; the launch traced here: 456 us
  waiting for transfers between devices  238 us (52%)
  blocking collectives  131 us (29%)
  matrix products  21.4 us (5%)
  local copies, waits for them, and re-layouts  20 us (4%)
  other arithmetic  19.1 us (4%)
  between operations  15.3 us (3%)
  starting transfers between devices  10.8 us (2%)
    unnamed x1, blocking collectives  131 us
    all_gather x1, waiting for transfers between devices, entering(): gathered = jax.tree.map(lambda a: lax.all_gather(a, axis), part)  99.1 us
    all_gather x1, waiting for transfers between devices, on_device(): lax.all_gather(output_weight, 'seq', axis=1, tiled=True)  78.8 us
    reduce_scatter x1, waiting for transfers between devices, on_device(): lax.psum_scatter(partial_value, 'head', scatter_dimension=1, tiled=True)  59.2 us
    dot_general x1, matrix products, on_device(): jnp.dot(normed, lax.all_gather(output_weight, 'seq', axis=1, tiled=True),...  13.1 us
    ppermute x3, starting transfers between devices, passed_along(): lax.ppermute(value, axis, [(source, source + steps) for source in range(i...  10.8 us
  transfers between devices with their start and end apart: 6, of which 3 were waited for; matrix products, arithmetic and copies ran while one was open for 8% of the time, Pallas kernels for 0%

commit v1 on v0

--- a/solution.py
+++ b/solution.py
@@ -8,22 +8,12 @@
 GROUPS = 8
 INNER = 8192
 KERNEL = 4
+SPAN = 256
+DOC_MOST = 1536
+REACH = -(-(DOC_MOST - 1) // SPAN)
 
 
 highest = lax.Precision.HIGHEST
-
-
-def entering(part, axis, combine, identity):
-    place = lax.axis_index(axis)
-    gathered = jax.tree.map(lambda a: lax.all_gather(a, axis), part)
-    state = jax.tree.map(lambda a, e: jnp.zeros_like(a) + jnp.asarray(e, a.dtype), part, identity)
-
-    def one(step, state):
-        return combine(
-            state, jax.tree.map(lambda a: lax.dynamic_index_in_dim(a, step, 0, False), gathered)
-        )
-
-    return lax.fori_loop(0, place, one, state)
 
 
 def passed_along(value, axis, steps):
@@ -85,13 +75,12 @@
     return normed.astype(jnp.bfloat16)
 
 
-def chain_states(through, local_state):
-
-    def combine_pair(earlier, later):
-        return (earlier[0] * later[0], later[0][:, None, None] * earlier[1] + later[1])
-
-    neutral = (jnp.ones_like(through), jnp.zeros_like(local_state))
-    return entering((through, local_state), "seq", combine_pair, neutral)[1]
+def chain_states(fading, deposit):
+    carried = passed_along(deposit.astype(jnp.bfloat16), "seq", 1)
+    for _ in range(REACH - 1):
+        held = fading[:, None, None] * carried.astype(jnp.float32) + deposit
+        carried = passed_along(held.astype(jnp.bfloat16), "seq", 1)
+    return carried.astype(jnp.float32)
 
 
 def on_device(
@@ -107,6 +96,7 @@
     norm_gain,
     output_weight,
 ):
+    weight = lax.all_gather(output_weight, "seq", axis=1, tiled=True)
     margin = KERNEL - 1
     length = documents.shape[0]
     head_count = decay_exponent.shape[0]
@@ -131,28 +121,16 @@
     decay_rate = -step_size * jnp.exp(decay_exponent)[:, None]
     skipped = skip_gain[None, :, None] * values.astype(jnp.float32)
     prior_segment = segments_wide[margin - 1]
-    pieces = [
-        span_parts(values, write_rows, read_rows, step_size, decay_rate, documents, prior_segment)
-    ]
-    local_state = jnp.zeros((head_count, HEAD_DIM, STATE), jnp.float32)
-    through = jnp.ones((head_count,), jnp.float32)
-    block_index = 0
-    within, inflow, fading, deposit = pieces[block_index]
-    local_state = fading[:, None, None] * local_state + deposit
-    through = through * fading
-    carried = chain_states(through, local_state)
-    block_index = 0
-    within, inflow, fading, deposit = pieces[block_index]
+    within, inflow, fading, deposit = span_parts(
+        values, write_rows, read_rows, step_size, decay_rate, documents, prior_segment
+    )
+    carried = chain_states(fading, deposit)
     outputs = within + inflow.T[:, :, None] * reading(read_rows, carried, repeat) + skipped
     scan_out = outputs.reshape(length, head_count * HEAD_DIM)
     normed = gated_norm(scan_out, gate_input, norm_gain)
-    partial_value = jnp.dot(
-        normed,
-        lax.all_gather(output_weight, "seq", axis=1, tiled=True),
-        preferred_element_type=jnp.float32,
-    )
-    return lax.psum_scatter(partial_value, "head", scatter_dimension=1, tiled=True).astype(
-        jnp.bfloat16
+    partial_value = jnp.dot(normed, weight, preferred_element_type=jnp.float32)
+    return lax.psum_scatter(
+        partial_value.astype(jnp.bfloat16), "head", scatter_dimension=1, tiled=True
     )
 
 

time: 459 us -> 201 us (0.44)
  waiting for transfers between devices: 238 us -> 101 us
  blocking collectives: 131 us -> 0 us
  starting transfers between devices: 10.8 us -> 34.9 us
  matrix products: 21.4 us -> 14.7 us
    all_gather x2 -> x1, waiting for transfers between devices: 178 us -> 0.01 us  [on_device(): weight = lax.all_gather(output_weight, 'seq', axis=1, tiled=True)]
    unnamed x1 -> x0, blocking collectives: 131 us -> none
    ppermute x3 -> x9, waiting for transfers between devices: 0.01 us -> 64.8 us  [passed_along(): lax.ppermute(value, axis, [(source, source + steps) for source in range(i...]
    ppermute x3 -> x9, starting transfers between devices: 10.8 us -> 34.9 us  [passed_along(): lax.ppermute(value, axis, [(source, source + steps) for source in range(i...]
    reduce_scatter x1, waiting for transfers between devices: 59.2 us -> 35.8 us  [on_device(): lax.psum_scatter(partial_value.astype(jnp.bfloat16), 'head', scatter_dime...]
  transfers between devices with their start and end apart: 6 -> 11, of which waited for: 3 -> 7; matrix products, arithmetic and copies ran while one was open for 8% -> 19% of each run, Pallas kernels for 0% -> 0%
where the time goes in v1:
time: 201 us; the launch traced here: 200 us
  waiting for transfers between devices  101 us (50%)
  starting transfers between devices  34.9 us (17%)
  local copies, waits for them, and re-layouts  17.9 us (9%)
  other arithmetic  16.2 us (8%)
  between operations  15 us (7%)
  matrix products  14.7 us (7%)
    ppermute x9, waiting for transfers between devices, passed_along(): lax.ppermute(value, axis, [(source, source + steps) for source in range(i...  64.8 us
    reduce_scatter x1, waiting for transfers between devices, on_device(): lax.psum_scatter(partial_value.astype(jnp.bfloat16), 'head', scatter_dime...  35.8 us
    ppermute x9, starting transfers between devices, passed_along(): lax.ppermute(value, axis, [(source, source + steps) for source in range(i...  34.9 us
    dot_general x1, matrix products, on_device(): partial_value = jnp.dot(normed, weight, preferred_element_type=jnp.float32)  10.3 us
  transfers between devices with their start and end apart: 11, of which 7 were waited for; matrix products, arithmetic and copies ran while one was open for 19% of the time, Pallas kernels for 0%

profile of v1, /device:TPU:1, one launch (start us, length us, event | category | flops | bytes accessed | tf_op | source)
XLA Modules:
  0.0 200.1 jit_solution(3075125419271925452)
XLA Ops:
  8.1 4.9 %collective-permute-start = (bf16[3]{0:T(256)(128)(2,1)S(1)}, bf16[3]{0:T(256)(128)(2,1)S(1)}, u32[]{:S(2)}, u32[]{:S(2)}) collective-permute-start(bf16[3]{0:T(256)(128)(2,1)S(1)} %slice.86), channel_id=1, source_target_pairs={{0,4},{4,8},{8,12},{12,16},{16,20},{20,24},{24,28},{28,32},{32,36}... | collective-permute-start | bytes 26 | tf_op jit(solution)/shard_map/ppermute | solution.py:22
  13.9 1.9 collective-permute-start.2
  16.6 3.9 %collective-permute-start.1 = (bf16[3,2048]{1,0:T(4,128)(2,1)S(1)}, bf16[3,2048]{1,0:T(4,128)(2,1)S(1)}, u32[]{:S(2)}, u32[]{:S(2)}) collective-permute-start(bf16[3,2048]{1,0:T(4,128)(2,1)S(1)} %slice.88), channel_id=1, source_target_pairs={{0,4},{4,8},{8,12},{12,16},{16,20},{20,24},{24,28},{28,32},{32,36}... | collective-permute-start | bytes 36872 | tf_op jit(solution)/shard_map/ppermute | solution.py:22
  20.5 1.2 slice.112
  21.7 1.1 copy.42
  23.5 0.8 copy_bitcast_fusion.1
  26.1 0.9 fusion.21
  28.4 1.9 slice_compare_fusion.2
  30.4 0.8 multiply_bitcast_fusion.1
  32.2 2.1 %multiply_convert_fusion.1 = bf16[256,2048]{1,0:T(8,128)(2,1)S(1)} fusion(bf16[256,2048]{1,0:T(8,128)(2,1)S(1)} %copy-done, bf16[3,2048]{1,0:T(4,128)(2,1)S(1)} %collective-permute-done.1, f32[2048]{0:T(1024)S(1)} %bitcast.77, f32[2048]{0:T(1024)S(1)} %bitcast.78, f32[2048]{0:T(1024)S(1)} %bitcast.76, f32[2048]{0:T(1024)S(1)} %bitcast.75, ...), kind=kLoop, calls=%fused_computation.17 | loop fusion | flops 14680064 | bytes 2142976 | tf_op jit(solution)/shard_map/convert_element_type | solution.py:33
  35.8 1.9 collective-permute-start.3
  39.0 9.4 %collective-permute-done.3 = bf16[32,64,128]{2,1,0:T(8,128)(2,1)S(1)} collective-permute-done((bf16[32,64,128]{2,1,0:T(8,128)(2,1)S(1)}, bf16[32,64,128]{2,1,0:T(8,128)(2,1)S(1)}, u32[]{:S(2)}, u32[]{:S(2)}) %collective-permute-start.3) | collective-permute-done | bytes 524320 | tf_op jit(solution)/shard_map/ppermute | solution.py:22
  48.5 4.5 %collective-permute-start.4 = (bf16[32,64,128]{2,1,0:T(8,128)(2,1)S(1)}, bf16[32,64,128]{2,1,0:T(8,128)(2,1)S(1)}, u32[]{:S(2)}, u32[]{:S(2)}) collective-permute-start(bf16[32,64,128]{2,1,0:T(8,128)(2,1)S(1)} %add_convert_fusion.4), channel_id=1, source_target_pairs={{0,4},{4,8},{8,12},{12,16},{16,20},{20,24},{24,28},{28,32},{32,36}... | collective-permute-start | bytes 1572872 | tf_op jit(solution)/shard_map/ppermute | solution.py:22
  53.0 6.3 %collective-permute-done.4 = bf16[32,64,128]{2,1,0:T(8,128)(2,1)S(1)} collective-permute-done((bf16[32,64,128]{2,1,0:T(8,128)(2,1)S(1)}, bf16[32,64,128]{2,1,0:T(8,128)(2,1)S(1)}, u32[]{:S(2)}, u32[]{:S(2)}) %collective-permute-start.4) | collective-permute-done | bytes 524320 | tf_op jit(solution)/shard_map/ppermute | solution.py:22
  59.5 4.4 %collective-permute-start.5 = (bf16[32,64,128]{2,1,0:T(8,128)(2,1)S(1)}, bf16[32,64,128]{2,1,0:T(8,128)(2,1)S(1)}, u32[]{:S(2)}, u32[]{:S(2)}) collective-permute-start(bf16[32,64,128]{2,1,0:T(8,128)(2,1)S(1)} %add_convert_fusion.3), channel_id=1, source_target_pairs={{0,4},{4,8},{8,12},{12,16},{16,20},{20,24},{24,28},{28,32},{32,36}... | collective-permute-start | bytes 1572872 | tf_op jit(solution)/shard_map/ppermute | solution.py:22
  63.9 16.7 %collective-permute-done.5 = bf16[32,64,128]{2,1,0:T(8,128)(2,1)S(1)} collective-permute-done((bf16[32,64,128]{2,1,0:T(8,128)(2,1)S(1)}, bf16[32,64,128]{2,1,0:T(8,128)(2,1)S(1)}, u32[]{:S(2)}, u32[]{:S(2)}) %collective-permute-start.5) | collective-permute-done | bytes 524320 | tf_op jit(solution)/shard_map/ppermute | solution.py:22
  80.8 4.4 %collective-permute-start.6 = (bf16[32,64,128]{2,1,0:T(8,128)(2,1)S(1)}, bf16[32,64,128]{2,1,0:T(8,128)(2,1)S(1)}, u32[]{:S(2)}, u32[]{:S(2)}) collective-permute-start(bf16[32,64,128]{2,1,0:T(8,128)(2,1)S(1)} %add_convert_fusion.2), channel_id=1, source_target_pairs={{0,4},{4,8},{8,12},{12,16},{16,20},{20,24},{24,28},{28,32},{32,36}... | collective-permute-start | bytes 1572872 | tf_op jit(solution)/shard_map/ppermute | solution.py:22
  85.2 17.3 %collective-permute-done.6 = bf16[32,64,128]{2,1,0:T(8,128)(2,1)S(1)} collective-permute-done((bf16[32,64,128]{2,1,0:T(8,128)(2,1)S(1)}, bf16[32,64,128]{2,1,0:T(8,128)(2,1)S(1)}, u32[]{:S(2)}, u32[]{:S(2)}) %collective-permute-start.6) | collective-permute-done | bytes 524320 | tf_op jit(solution)/shard_map/ppermute | solution.py:22
  102.7 4.4 %collective-permute-start.7 = (bf16[32,64,128]{2,1,0:T(8,128)(2,1)S(1)}, bf16[32,64,128]{2,1,0:T(8,128)(2,1)S(1)}, u32[]{:S(2)}, u32[]{:S(2)}) collective-permute-start(bf16[32,64,128]{2,1,0:T(8,128)(2,1)S(1)} %add_convert_fusion.1), channel_id=1, source_target_pairs={{0,4},{4,8},{8,12},{12,16},{16,20},{20,24},{24,28},{28,32},{32,36}... | collective-permute-start | bytes 1572872 | tf_op jit(solution)/shard_map/ppermute | solution.py:22
  107.2 13.3 %collective-permute-done.7 = bf16[32,64,128]{2,1,0:T(8,128)(2,1)S(1)} collective-permute-done((bf16[32,64,128]{2,1,0:T(8,128)(2,1)S(1)}, bf16[32,64,128]{2,1,0:T(8,128)(2,1)S(1)}, u32[]{:S(2)}, u32[]{:S(2)}) %collective-permute-start.7) | collective-permute-done | bytes 524320 | tf_op jit(solution)/shard_map/ppermute | solution.py:22
  120.8 4.6 %collective-permute-start.8 = (bf16[32,64,128]{2,1,0:T(8,128)(2,1)S(1)}, bf16[32,64,128]{2,1,0:T(8,128)(2,1)S(1)}, u32[]{:S(2)}, u32[]{:S(2)}) collective-permute-start(bf16[32,64,128]{2,1,0:T(8,128)(2,1)S(1)} %add_convert_fusion), channel_id=1, source_target_pairs={{0,4},{4,8},{8,12},{12,16},{16,20},{20,24},{24,28},{28,32},{32,36}... | collective-permute-start | bytes 1572872 | tf_op jit(solution)/shard_map/ppermute | solution.py:22
  125.8 2.3 %fusion.1 = bf16[32,256,256]{2,1,0:T(8,128)(2,1)S(1)} fusion(f32[32,256]{1,0:T(8,128)S(1)} %get-tuple-element.9, f32[2,256,256]{2,1,0:T(8,128)S(1)} %fusion.23, f32[32,256]{1,0:T(8,128)S(1)} %copy_bitcast_fusion, pred[256,256]{1,0:T(8,128)(4,1)S(1)} %fusion.17), kind=kLoop, calls=%fused_computation.2 | loop fusion | flops 10485760 | bytes 4849664 | tf_op jit(solution)/shard_map/convert_element_type | solution.py:48
  128.1 1.4 fusion.24
  129.5 1.8 collective-permute-done.8
  131.8 2.2 %fusion.3 = f32[256,32,64]{0,2,1:T(8,128)} fusion(bf16[256,32,64]{0,2,1:T(8,128)(2,1)S(1)} %bitcast.65, f32[32,64,256]{2,1,0:T(8,128)S(1)} %fusion.24, bf16[32,64,128]{2,1,0:T(8,128)(2,1)S(1)} %collective-permute-done.8, bf16[256,32,128]{2,0,1:T(8,128)(2,1)S(1)} %bitcast.68, f32[32]{0:T(128)S(1)} %copy-done.3, f32[256,32]{0,1:T(8,128)S(1)} %get-tuple-element.7), kind=kOutput, calls=%fused_computation.9 | convolution fusion | flops 136839168 | bytes 7897216 | tf_op jit(solution)/shard_map/ihn,hpn->ihp/dot_general | solution.py:66
  134.0 2.0 %copy.48 = f32[256,2048]{1,0:T(8,128)S(1)} copy(f32[256,2048]{0,1:T(8,128)} %bitcast.69) | data formatting | bytes 4194304 | tf_op jit(solution)/shard_map/reshape | solution.py:129
  136.0 1.9 fusion.19
  138.0 4.0 %mul.276 = f32[256,2,1024]{2,1,0:T(2,128)} reshape(f32[256,2048]{1,0:T(8,128)} %fusion.19) | data formatting | bytes 4194304 | tf_op jit(solution)/shard_map/mul | solution.py:73
  142.0 2.2 %reduce_sum.9 = f32[256,2]{1,0:T(8,128)S(1)} reduce(f32[256,2,1024]{2,1,0:T(2,128)} %mul.276, f32[]{:T(128)} %constant.8.clone.1), dimensions={2}, to_apply=%region_2.3 | reduce | flops 523776 | bytes 2099204 | tf_op jit(solution)/shard_map/reduce_sum | solution.py:73
  144.8 2.2 %copy.55 = f32[32,8,2,1024]{3,1,2,0:T(8,128)} copy(f32[32,8,2,1024]{3,2,1,0:T(2,128)S(1)} %bitcast.67) | data formatting | bytes 4194304
  147.1 10.3 %convolution_convert_fusion = bf16[256,4096]{1,0:T(8,128)(2,1)} fusion(bf16[2048,4096]{0,1:T(8,128)(2,1)} %all-gather.2.cloned.1.call-done, f32[256,2048]{1,0:T(8,128)} %bitcast.70, f32[2048]{0:T(1024)S(1)} %copy-done.4, f32[256,2048]{1,0:T(8,128)S(1)} %copy.48, bf16[256,2048]{1,0:T(8,128)(2,1)S(1)} %copy-done.1), kind=kOutput, calls=%fused_computation.3 | convolution fusion | flops 4300734464 | bytes 24125440 | tf_op jit(solution)/shard_map/dot_general | solution.py:131
  157.4 35.8 %reduce-scatter.2.cloned.1.call-done = bf16[256,1024]{1,0:T(8,128)(2,1)} async-done(((bf16[256,4096]{1,0:T(8,128)(2,1)}), bf16[256,1024]{1,0:T(8,128)(2,1)}) %reduce-scatter.2.cloned.1.call-update) | async-done | bytes 524304 | tf_op jit(solution)/shard_map/reduce_scatter | solution.py:132
  (52 shorter events, 11.9 us)
Async XLA Ops:
  6.5 25.6 %copy-start = (bf16[256,2048]{1,0:T(8,128)(2,1)S(1)}, bf16[256,2048]{1,0:T(8,128)(2,1)}, u32[]{:S(2)}) copy-start(bf16[256,2048]{1,0:T(8,128)(2,1)} %param.11) | copy-start | bytes 3145732
  6.5 140.5 %all-gather.2.cloned.1.call-start = ((), (), s32[]{:S(2)}) async-start(), calls=%async_computation.1 | async-start | bytes 17039360 | tf_op jit(solution)/shard_map/all_gather | solution.py:99
  7.3 186.0 %reduce-scatter.2.cloned.1.call-start = ((), (), s32[]{:S(2)}) async-start(), calls=%async_computation.2 | async-start | bytes 2621440 | tf_op jit(solution)/shard_map/reduce_scatter | solution.py:132
  8.1 19.0 %collective-permute-start = (bf16[3]{0:T(256)(128)(2,1)S(1)}, bf16[3]{0:T(256)(128)(2,1)S(1)}, u32[]{:S(2)}, u32[]{:S(2)}) collective-permute-start(bf16[3]{0:T(256)(128)(2,1)S(1)} %slice.86), channel_id=1, source_target_pairs={{0,4},{4,8},{8,12},{12,16},{16,20},{20,24},{24,28},{28,32},{32,36}... | collective-permute-start | bytes 26 | tf_op jit(solution)/shard_map/ppermute | solution.py:22
  13.9 17.4 %collective-permute-start.2 = (bf16[3,2,256]{0,2,1:T(8,128)(2,1)S(1)}, bf16[3,2,256]{0,2,1:T(8,128)(2,1)S(1)}, u32[]{:S(2)}, u32[]{:S(2)}) collective-permute-start(bf16[3,2,256]{0,2,1:T(8,128)(2,1)S(1)} %copy.41), channel_id=1, source_target_pairs={{0,4},{4,8},{8,12},{12,16},{16,20},{20,24},{24,28},{28,32},{32,36}... | collective-permute-start | bytes 9224 | tf_op jit(solution)/shard_map/ppermute | solution.py:22
  16.6 15.6 %collective-permute-start.1 = (bf16[3,2048]{1,0:T(4,128)(2,1)S(1)}, bf16[3,2048]{1,0:T(4,128)(2,1)S(1)}, u32[]{:S(2)}, u32[]{:S(2)}) collective-permute-start(bf16[3,2048]{1,0:T(4,128)(2,1)S(1)} %slice.88), channel_id=1, source_target_pairs={{0,4},{4,8},{8,12},{12,16},{16,20},{20,24},{24,28},{28,32},{32,36}... | collective-permute-start | bytes 36872 | tf_op jit(solution)/shard_map/ppermute | solution.py:22
  35.8 12.5 %collective-permute-start.3 = (bf16[32,64,128]{2,1,0:T(8,128)(2,1)S(1)}, bf16[32,64,128]{2,1,0:T(8,128)(2,1)S(1)}, u32[]{:S(2)}, u32[]{:S(2)}) collective-permute-start(bf16[32,64,128]{2,1,0:T(8,128)(2,1)S(1)} %get-tuple-element.23), channel_id=1, source_target_pairs={{0,4},{4,8},{8,12},{12,16},{16,20},{20,24},{24,28},{28,32},{32,36}... | collective-permute-start | bytes 1572872 | tf_op jit(solution)/shard_map/ppermute | solution.py:22
  48.5 10.8 %collective-permute-start.4 = (bf16[32,64,128]{2,1,0:T(8,128)(2,1)S(1)}, bf16[32,64,128]{2,1,0:T(8,128)(2,1)S(1)}, u32[]{:S(2)}, u32[]{:S(2)}) collective-permute-start(bf16[32,64,128]{2,1,0:T(8,128)(2,1)S(1)} %add_convert_fusion.4), channel_id=1, source_target_pairs={{0,4},{4,8},{8,12},{12,16},{16,20},{20,24},{24,28},{28,32},{32,36}... | collective-permute-start | bytes 1572872 | tf_op jit(solution)/shard_map/ppermute | solution.py:22
  59.5 47.6 %copy-start.2 = (s32[256]{0:T(256)S(1)}, s32[256]{0:T(256)}, u32[]{:S(2)}) copy-start(s32[256]{0:T(256)} %param.17) | copy-start | bytes 3076
  59.5 21.1 %collective-permute-start.5 = (bf16[32,64,128]{2,1,0:T(8,128)(2,1)S(1)}, bf16[32,64,128]{2,1,0:T(8,128)(2,1)S(1)}, u32[]{:S(2)}, u32[]{:S(2)}) collective-permute-start(bf16[32,64,128]{2,1,0:T(8,128)(2,1)S(1)} %add_convert_fusion.3), channel_id=1, source_target_pairs={{0,4},{4,8},{8,12},{12,16},{16,20},{20,24},{24,28},{28,32},{32,36}... | collective-permute-start | bytes 1572872 | tf_op jit(solution)/shard_map/ppermute | solution.py:22
  80.8 21.7 %collective-permute-start.6 = (bf16[32,64,128]{2,1,0:T(8,128)(2,1)S(1)}, bf16[32,64,128]{2,1,0:T(8,128)(2,1)S(1)}, u32[]{:S(2)}, u32[]{:S(2)}) collective-permute-start(bf16[32,64,128]{2,1,0:T(8,128)(2,1)S(1)} %add_convert_fusion.2), channel_id=1, source_target_pairs={{0,4},{4,8},{8,12},{12,16},{16,20},{20,24},{24,28},{28,32},{32,36}... | collective-permute-start | bytes 1572872 | tf_op jit(solution)/shard_map/ppermute | solution.py:22
  102.7 17.9 %collective-permute-start.7 = (bf16[32,64,128]{2,1,0:T(8,128)(2,1)S(1)}, bf16[32,64,128]{2,1,0:T(8,128)(2,1)S(1)}, u32[]{:S(2)}, u32[]{:S(2)}) collective-permute-start(bf16[32,64,128]{2,1,0:T(8,128)(2,1)S(1)} %add_convert_fusion.1), channel_id=1, source_target_pairs={{0,4},{4,8},{8,12},{12,16},{16,20},{20,24},{24,28},{28,32},{32,36}... | collective-permute-start | bytes 1572872 | tf_op jit(solution)/shard_map/ppermute | solution.py:22
  120.8 10.5 %collective-permute-start.8 = (bf16[32,64,128]{2,1,0:T(8,128)(2,1)S(1)}, bf16[32,64,128]{2,1,0:T(8,128)(2,1)S(1)}, u32[]{:S(2)}, u32[]{:S(2)}) collective-permute-start(bf16[32,64,128]{2,1,0:T(8,128)(2,1)S(1)} %add_convert_fusion), channel_id=1, source_target_pairs={{0,4},{4,8},{8,12},{12,16},{16,20},{20,24},{24,28},{28,32},{32,36}... | collective-permute-start | bytes 1572872 | tf_op jit(solution)/shard_map/ppermute | solution.py:22
  129.4 2.3 %copy-start.3 = (f32[32]{0:T(128)S(1)}, f32[32]{0:T(128)}, u32[]{:S(2)}) copy-start(f32[32]{0:T(128)} %param.16) | copy-start | bytes 388
  134.0 2.0 %copy-start.1 = (bf16[256,2048]{1,0:T(8,128)(2,1)S(1)}, bf16[256,2048]{1,0:T(8,128)(2,1)}, u32[]{:S(2)}) copy-start(bf16[256,2048]{1,0:T(8,128)(2,1)} %param.13) | copy-start | bytes 3145732
  144.8 2.2 %copy-start.4 = (f32[2048]{0:T(1024)S(1)}, f32[2048]{0:T(1024)}, u32[]{:S(2)}) copy-start(f32[2048]{0:T(1024)} %param.20) | copy-start | bytes 24580
Sparse Core Ops, SparseCore 0:
  10.1 112.5 all-gather.1
  157.5 35.6 reduce-scatter.1

commit v2 on v1

--- a/solution.py
+++ b/solution.py
@@ -67,20 +67,47 @@
 
 
 def gated_norm(outputs, gates, norm_scale):
-    height = outputs.shape[0]
+    width = INNER // GROUPS
     gated = outputs * jax.nn.silu(gates.astype(jnp.float32))
-    grouped = gated.reshape(height, -1, INNER // GROUPS)
-    mean_square = jnp.mean(grouped * grouped, axis=-1, keepdims=True)
-    normed = (grouped * lax.rsqrt(mean_square + 1e-05)).reshape(height, -1) * norm_scale
-    return normed.astype(jnp.bfloat16)
+    pieces = []
+    for start in range(0, outputs.shape[1], width):
+        group = gated[:, start : start + width]
+        mean_square = jnp.mean(group * group, axis=-1, keepdims=True)
+        scaled = group * lax.rsqrt(mean_square + 1e-05) * norm_scale[start : start + width]
+        pieces.append(scaled.astype(jnp.bfloat16))
+    return jnp.concatenate(pieces, axis=1)
 
 
 def chain_states(fading, deposit):
-    carried = passed_along(deposit.astype(jnp.bfloat16), "seq", 1)
-    for _ in range(REACH - 1):
-        held = fading[:, None, None] * carried.astype(jnp.float32) + deposit
-        carried = passed_along(held.astype(jnp.bfloat16), "seq", 1)
-    return carried.astype(jnp.float32)
+    half = fading.shape[0] // 2
+    count = lax.axis_size("seq")
+    swap = [(place, place ^ 1) for place in range(count)]
+    second = lax.axis_index("seq") % 2 == 1
+
+    def own(a):
+        return jnp.where(second, a[half:], a[:half])
+
+    def partner(a):
+        return jnp.where(second, a[:half], a[half:])
+
+    there = own(lax.ppermute(fading, "seq", swap))[:, None, None]
+    here = own(fading)[:, None, None]
+    other = lax.ppermute(partner(deposit).astype(jnp.bfloat16), "seq", swap).astype(jnp.float32)
+    mine = own(deposit)
+    early_fade, late_fade = jnp.where(second, there, here), jnp.where(second, here, there)
+    early, late = jnp.where(second, other, mine), jnp.where(second, mine, other)
+    added = late_fade * early + late
+    scale = early_fade * late_fade
+    carried = passed_along(added.astype(jnp.bfloat16), "seq", 2)
+    for _ in range(-(-REACH // 2) - 1):
+        held = scale * carried.astype(jnp.float32) + added
+        carried = passed_along(held.astype(jnp.bfloat16), "seq", 2)
+    first = carried.astype(jnp.float32)
+    between = early_fade * first + early
+    sent = jnp.where(second, first, between).astype(jnp.bfloat16)
+    kept = jnp.where(second, between, first)
+    got = lax.ppermute(sent, "seq", swap).astype(jnp.float32)
+    return jnp.concatenate([jnp.where(second, got, kept), jnp.where(second, kept, got)])
 
 
 def on_device(
@@ -102,11 +129,20 @@
     head_count = decay_exponent.shape[0]
     groups = state_input.shape[2] // STATE
     repeat = head_count // groups
-    before_inner, before_state, before_segments = passed_along(
-        (inner_input[-margin:], state_input[-margin:], documents[-margin:].astype(jnp.bfloat16)),
-        "seq",
-        1,
+    channels = inner_input.shape[1]
+    state_channels = 2 * state_input.shape[2]
+    halo = jnp.concatenate(
+        [
+            inner_input[-margin:],
+            state_input[-margin:].reshape(margin, state_channels),
+            jnp.broadcast_to(documents[-margin:, None].astype(jnp.bfloat16), (margin, 128)),
+        ],
+        axis=1,
     )
+    halo = passed_along(halo, "seq", 1)
+    before_inner = halo[:, :channels]
+    before_state = halo[:, channels : channels + state_channels].reshape(margin, 2, -1)
+    before_segments = halo[:, channels + state_channels]
     segments_wide = jnp.concatenate([before_segments.astype(jnp.int32), documents])
     inner_conv = causal_conv(
         jnp.concatenate([before_inner, inner_input]), filter_inner, segments_wide, documents

time: 201 us -> 171 us (0.85)
  waiting for transfers between devices: 101 us -> 82.4 us
  starting transfers between devices: 34.9 us -> 24.1 us
  matrix products: 14.7 us -> 23.8 us
  local copies, waits for them, and re-layouts: 17.9 us -> 11.4 us
  other arithmetic: 16.2 us -> 13.4 us
    ppermute x9 -> x4, waiting for transfers between devices: 64.8 us -> 15.5 us  [passed_along(): lax.ppermute(value, axis, [(source, source + steps) for source in range(i...]
    all_gather x1, waiting for transfers between devices: 0.01 us -> 35.4 us  [on_device(): weight = lax.all_gather(output_weight, 'seq', axis=1, tiled=True)]
    ppermute x9 -> x4, starting transfers between devices: 34.9 us -> 17 us  [passed_along(): lax.ppermute(value, axis, [(source, source + steps) for source in range(i...]
    dot_general x1, matrix products: 10.3 us -> 18.1 us  [on_device(): partial_value = jnp.dot(normed, weight, preferred_element_type=jnp.float32)]
    ppermute x0 -> x3, starting transfers between devices: none -> 7.1 us  [the longest x1 6.52 us: chain_states(): got = lax.ppermute(sent, 'seq', swap).astype(jnp.float32)]
    reduce_scatter x1, waiting for transfers between devices: 35.8 us -> 29.8 us  [on_device(): lax.psum_scatter(partial_value.astype(jnp.bfloat16), 'head', scatter_dime...]
    mul x2 -> x0, local copies, waits for them, and re-layouts: 4.6 us -> none  [the longest x1 4 us: gated_norm(): mean_square = jnp.mean(grouped * grouped, axis=-1, keepdims=True)]
  transfers between devices with their start and end apart: 11 -> 9, of which waited for: 7 -> 6; matrix products, arithmetic and copies ran while one was open for 19% -> 18% of each run, Pallas kernels for 0% -> 0%
where the time goes in v2:
time: 171 us; the launch traced here: 170 us
  waiting for transfers between devices  82.4 us (48%)
  starting transfers between devices  24.1 us (14%)
  matrix products  23.8 us (14%)
  between operations  15.1 us (9%)
  other arithmetic  13.4 us (8%)
  local copies, waits for them, and re-layouts  11.4 us (7%)
    all_gather x1, waiting for transfers between devices, on_device(): weight = lax.all_gather(output_weight, 'seq', axis=1, tiled=True)  35.4 us
    reduce_scatter x1, waiting for transfers between devices, on_device(): lax.psum_scatter(partial_value.astype(jnp.bfloat16), 'head', scatter_dime...  29.8 us
    dot_general x1, matrix products, on_device(): partial_value = jnp.dot(normed, weight, preferred_element_type=jnp.float32)  18.1 us
    ppermute x4, starting transfers between devices, passed_along(): lax.ppermute(value, axis, [(source, source + steps) for source in range(i...  17 us
    ppermute x4, waiting for transfers between devices, passed_along(): lax.ppermute(value, axis, [(source, source + steps) for source in range(i...  15.5 us
    ppermute x1, starting transfers between devices, chain_states(): got = lax.ppermute(sent, 'seq', swap).astype(jnp.float32)  6.52 us
    dot_general x1, matrix products, reading(): return jnp.einsum('ihn,hpn->ihp', readers, held_state, precision=highest)  3.64 us
  transfers between devices with their start and end apart: 9, of which 6 were waited for; matrix products, arithmetic and copies ran while one was open for 18% of the time, Pallas kernels for 0%

profile of v2, /device:TPU:1, one launch (start us, length us, event | category | flops | bytes accessed | tf_op | source)
XLA Modules:
  0.0 170.2 jit_solution(2397949163513260238)
XLA Ops:
  6.5 0.7 all-gather.2.cloned.1.call-update
  7.3 0.8 slice.128
  8.1 0.7 slice_bitcast_fusion
  8.8 0.7 convert.3
  9.6 4.9 %collective-permute-start = (bf16[3,2688]{1,0:T(4,128)(2,1)S(1)}, bf16[3,2688]{1,0:T(4,128)(2,1)S(1)}, u32[]{:S(2)}, u32[]{:S(2)}) collective-permute-start(bf16[3,2688]{1,0:T(4,128)(2,1)S(1)} %pad_maximum_fusion.2), channel_id=1, source_target_pairs={{0,4},{4,8},{8,12},{12,16},{16,20},{20,24},{24,28},{28,32},{32,36}... | collective-permute-start | bytes 48392 | tf_op jit(solution)/shard_map/ppermute | solution.py:22
  14.6 0.7 exp.32
  15.2 0.8 copy_bitcast_fusion.1
  16.1 0.6 reduce-window.6
  16.8 0.7 slice_bitcast_fusion.4
  17.7 0.9 fusion.32
  18.8 1.3 slice.157
  20.1 1.1 copy.19
  23.4 0.8 pad_add_fusion
  24.1 2.0 %slice_compare_fusion.2 = (pred[256]{0:T(512)(128)(4,1)S(1)}, pred[256]{0:T(512)(128)(4,1)S(1)}, pred[256]{0:T(512)(128)(4,1)S(1)}, f32[256]{0:T(256)S(1)}, f32[256]{0:T(256)S(1)}) fusion(s32[256]{0:T(256)} %param.17, s32[259]{0:T(512)S(1)} %pad_add_fusion, s32[]{:T(128)} %bitcast.14, s32[]{:T(128)} %bitcast.16), kind=kLoop, calls=%fused_computation.81 | loop fusion | flops 1792 | bytes 6920 | tf_op jit(solution)/shard_map/eq | solution.py:30
  26.1 0.7 multiply_convert_fusion.3
  27.1 2.1 %multiply_convert_fusion = bf16[256,2048]{1,0:T(8,128)(2,1)S(1)} fusion(bf16[256,2048]{1,0:T(8,128)(2,1)S(1)} %copy-done, bf16[3,2048]{1,0:T(4,128)(2,1)S(1)} %slice.169, f32[2048]{0:T(1024)S(1)} %bitcast.77, f32[2048]{0:T(1024)S(1)} %bitcast.78, f32[2048]{0:T(1024)S(1)} %bitcast.76, f32[2048]{0:T(1024)S(1)} %bitcast.75, ...), kind=kLoop, calls=%fused_computation.16 | loop fusion | flops 14680064 | bytes 2142976 | tf_op jit(solution)/shard_map/convert_element_type | solution.py:33
  29.8 0.7 multiply_bitcast_fusion.1
  32.1 1.0 collective-permute-done.1
  33.4 3.7 %collective-permute-start.3 = (bf16[16,64,128]{2,1,0:T(8,128)(2,1)S(1)}, bf16[16,64,128]{2,1,0:T(8,128)(2,1)S(1)}, u32[]{:S(2)}, u32[]{:S(2)}) collective-permute-start(bf16[16,64,128]{2,1,0:T(8,128)(2,1)S(1)} %get-tuple-element.9), channel_id=1, source_target_pairs={{0,8},{4,12},{8,16},{12,20},{16,24},{20,28},{24,32},{28,36},{32,40... | collective-permute-start | bytes 786440 | tf_op jit(solution)/shard_map/ppermute | solution.py:22
  37.1 9.5 %collective-permute-done.3 = bf16[16,64,128]{2,1,0:T(8,128)(2,1)S(1)} collective-permute-done((bf16[16,64,128]{2,1,0:T(8,128)(2,1)S(1)}, bf16[16,64,128]{2,1,0:T(8,128)(2,1)S(1)}, u32[]{:S(2)}, u32[]{:S(2)}) %collective-permute-start.3) | collective-permute-done | bytes 262176 | tf_op jit(solution)/shard_map/ppermute | solution.py:22
  46.8 4.2 %collective-permute-start.4 = (bf16[16,64,128]{2,1,0:T(8,128)(2,1)S(1)}, bf16[16,64,128]{2,1,0:T(8,128)(2,1)S(1)}, u32[]{:S(2)}, u32[]{:S(2)}) collective-permute-start(bf16[16,64,128]{2,1,0:T(8,128)(2,1)S(1)} %add_convert_fusion.1), channel_id=1, source_target_pairs={{0,8},{4,12},{8,16},{12,20},{16,24},{20,28},{24,32},{28,36},{32,40... | collective-permute-start | bytes 786440 | tf_op jit(solution)/shard_map/ppermute | solution.py:22
  51.2 5.1 %collective-permute-done.4 = bf16[16,64,128]{2,1,0:T(8,128)(2,1)S(1)} collective-permute-done((bf16[16,64,128]{2,1,0:T(8,128)(2,1)S(1)}, bf16[16,64,128]{2,1,0:T(8,128)(2,1)S(1)}, u32[]{:S(2)}, u32[]{:S(2)}) %collective-permute-start.4) | collective-permute-done | bytes 262176 | tf_op jit(solution)/shard_map/ppermute | solution.py:22
  56.5 4.1 %collective-permute-start.5 = (bf16[16,64,128]{2,1,0:T(8,128)(2,1)S(1)}, bf16[16,64,128]{2,1,0:T(8,128)(2,1)S(1)}, u32[]{:S(2)}, u32[]{:S(2)}) collective-permute-start(bf16[16,64,128]{2,1,0:T(8,128)(2,1)S(1)} %add_convert_fusion), channel_id=1, source_target_pairs={{0,8},{4,12},{8,16},{12,20},{16,24},{20,28},{24,32},{28,36},{32,40... | collective-permute-start | bytes 786440 | tf_op jit(solution)/shard_map/ppermute | solution.py:22
  61.1 2.4 %fusion.1 = bf16[32,256,256]{2,1,0:T(8,128)(2,1)S(1)} fusion(f32[32,256]{1,0:T(8,128)S(1)} %copy-done.5, f32[2,256,256]{2,1,0:T(8,128)S(1)} %fusion.34, f32[32,256]{1,0:T(8,128)S(1)} %copy-done.3, pred[256,256]{1,0:T(8,128)(4,1)S(1)} %fusion.25), kind=kLoop, calls=%fused_computation.2 | loop fusion | flops 10485760 | bytes 4849664 | tf_op jit(solution)/shard_map/convert_element_type | solution.py:48
  63.5 0.9 collective-permute-done.5
  64.5 6.5 %collective-permute-start.6 = (bf16[16,64,128]{2,1,0:T(8,128)(2,1)S(1)}, bf16[16,64,128]{2,1,0:T(8,128)(2,1)S(1)}, u32[]{:S(2)}, u32[]{:S(2)}) collective-permute-start(bf16[16,64,128]{2,1,0:T(8,128)(2,1)S(1)} %fusion.22), channel_id=1, source_target_pairs={{0,4},{4,0},{8,12},{12,8},{16,20},{20,16},{24,28},{28,24},{32,36},... | collective-permute-start | bytes 786440 | tf_op jit(solution)/shard_map/ppermute | solution.py:109
  71.0 1.4 fusion.35
  73.2 3.6 %fusion.3 = f32[256,32,64]{0,2,1:T(8,128)} fusion(bf16[256,32,64]{0,2,1:T(8,128)(2,1)S(1)} %bitcast.66, f32[32,64,256]{2,1,0:T(8,128)S(1)} %fusion.35, bf16[256,32,128]{2,0,1:T(8,128)(2,1)S(1)} %bitcast.68, f32[16,64,128]{2,1,0:T(8,128)S(1)} %get-tuple-element.14, f32[16,64,128]{2,1,0:T(8,128)S(1)} %get-tuple-element.13, f32[32]{0:T(128)S(1)} %copy-done.9, ...), kind=kOutput, calls=%fused_computation.9 | convolution fusion | flops 808189952 | bytes 8421504 | tf_op jit(solution)/shard_map/ihn,hpn->ihp/dot_general | solution.py:66
  76.8 2.2 %copy.25 = f32[256,2048]{1,0:T(8,128)S(1)} copy(f32[256,2048]{0,1:T(8,128)} %bitcast.69) | data formatting | bytes 4194304 | tf_op jit(solution)/shard_map/reshape | solution.py:165
  80.1 35.4 %all-gather.2.cloned.1.call-done = bf16[2048,4096]{0,1:T(8,128)(2,1)} async-done(((bf16[2048,64]{0,1:T(8,128)(2,1)}), bf16[2048,4096]{0,1:T(8,128)(2,1)}) %all-gather.2.cloned.1.call-update) | async-done | bytes 16777232 | tf_op jit(solution)/shard_map/all_gather | solution.py:126
  115.4 18.1 %convolution_convert_fusion = bf16[256,4096]{1,0:T(8,128)(2,1)} fusion(bf16[2048,4096]{0,1:T(8,128)(2,1)} %all-gather.2.cloned.1.call-done, bf16[256,1024]{1,0:T(8,128)(2,1)S(1)} %get-tuple-element.12, bf16[256,1024]{1,0:T(8,128)(2,1)S(1)} %get-tuple-element.11), kind=kOutput, calls=%fused_computation.3 | convolution fusion | flops 4298113024 | bytes 19922944 | tf_op jit(solution)/shard_map/dot_general | solution.py:167
  133.5 29.8 %reduce-scatter.2.cloned.1.call-done = bf16[256,1024]{1,0:T(8,128)(2,1)} async-done(((bf16[256,4096]{1,0:T(8,128)(2,1)}), bf16[256,1024]{1,0:T(8,128)(2,1)}) %reduce-scatter.2.cloned.1.call-update) | async-done | bytes 524304 | tf_op jit(solution)/shard_map/reduce_scatter | solution.py:168
  (65 shorter events, 6.9 us)
Async XLA Ops:
  6.5 20.5 %copy-start = (bf16[256,2048]{1,0:T(8,128)(2,1)S(1)}, bf16[256,2048]{1,0:T(8,128)(2,1)}, u32[]{:S(2)}) copy-start(bf16[256,2048]{1,0:T(8,128)(2,1)} %param.11) | copy-start | bytes 3145732
  6.5 108.9 %all-gather.2.cloned.1.call-start = ((), (), s32[]{:S(2)}) async-start(), calls=%async_computation.1 | async-start | bytes 17039360 | tf_op jit(solution)/shard_map/all_gather | solution.py:126
  7.3 156.1 %reduce-scatter.2.cloned.1.call-start = ((), (), s32[]{:S(2)}) async-start(), calls=%async_computation.2 | async-start | bytes 2621440 | tf_op jit(solution)/shard_map/reduce_scatter | solution.py:168
  9.6 11.6 %collective-permute-start = (bf16[3,2688]{1,0:T(4,128)(2,1)S(1)}, bf16[3,2688]{1,0:T(4,128)(2,1)S(1)}, u32[]{:S(2)}, u32[]{:S(2)}) collective-permute-start(bf16[3,2688]{1,0:T(4,128)(2,1)S(1)} %pad_maximum_fusion.2), channel_id=1, source_target_pairs={{0,4},{4,8},{8,12},{12,16},{16,20},{20,24},{24,28},{28,32},{32,36}... | collective-permute-start | bytes 48392 | tf_op jit(solution)/shard_map/ppermute | solution.py:22
  17.7 1.1 copy-start.2
  27.1 2.7 %copy-start.6 = (f32[32,256]{1,0:T(8,128)S(1)}, f32[32,256]{1,0:T(8,128)}, u32[]{:S(2)}) copy-start(f32[32,256]{1,0:T(8,128)} %param.14) | copy-start | bytes 98308
  31.4 19.6 %copy-start.7 = (s32[256]{0:T(256)S(1)}, s32[256]{0:T(256)}, u32[]{:S(2)}) copy-start(s32[256]{0:T(256)} %param.17) | copy-start | bytes 3076
  31.5 1.7 collective-permute-start.2
  31.6 1.5 collective-permute-start.1
  33.2 27.4 %copy-start.8 = (f32[2048]{0:T(1024)S(1)}, f32[2048]{0:T(1024)}, u32[]{:S(2)}) copy-start(f32[2048]{0:T(1024)} %param.20) | copy-start | bytes 24580
  33.4 27.7 %copy-start.3 = (f32[32,256]{1,0:T(8,128)S(1)}, f32[32,256]{1,0:T(8,128)}, u32[]{:S(2)}) copy-start(f32[32,256]{1,0:T(8,128)} %copy-done.2) | copy-start | bytes 98308
  33.4 27.7 %copy-start.5 = (f32[32,256]{1,0:T(8,128)S(1)}, f32[32,256]{1,0:T(8,128)}, u32[]{:S(2)}) copy-start(f32[32,256]{1,0:T(8,128)} %get-tuple-element.19) | copy-start | bytes 98308
  33.4 13.2 %collective-permute-start.3 = (bf16[16,64,128]{2,1,0:T(8,128)(2,1)S(1)}, bf16[16,64,128]{2,1,0:T(8,128)(2,1)S(1)}, u32[]{:S(2)}, u32[]{:S(2)}) collective-permute-start(bf16[16,64,128]{2,1,0:T(8,128)(2,1)S(1)} %get-tuple-element.9), channel_id=1, source_target_pairs={{0,8},{4,12},{8,16},{12,20},{16,24},{20,28},{24,32},{28,36},{32,40... | collective-permute-start | bytes 786440 | tf_op jit(solution)/shard_map/ppermute | solution.py:22
  46.8 9.5 %collective-permute-start.4 = (bf16[16,64,128]{2,1,0:T(8,128)(2,1)S(1)}, bf16[16,64,128]{2,1,0:T(8,128)(2,1)S(1)}, u32[]{:S(2)}, u32[]{:S(2)}) collective-permute-start(bf16[16,64,128]{2,1,0:T(8,128)(2,1)S(1)} %add_convert_fusion.1), channel_id=1, source_target_pairs={{0,8},{4,12},{8,16},{12,20},{16,24},{20,28},{24,32},{28,36},{32,40... | collective-permute-start | bytes 786440 | tf_op jit(solution)/shard_map/ppermute | solution.py:22
  56.5 7.8 %collective-permute-start.5 = (bf16[16,64,128]{2,1,0:T(8,128)(2,1)S(1)}, bf16[16,64,128]{2,1,0:T(8,128)(2,1)S(1)}, u32[]{:S(2)}, u32[]{:S(2)}) collective-permute-start(bf16[16,64,128]{2,1,0:T(8,128)(2,1)S(1)} %add_convert_fusion), channel_id=1, source_target_pairs={{0,8},{4,12},{8,16},{12,20},{16,24},{20,28},{24,32},{28,36},{32,40... | collective-permute-start | bytes 786440 | tf_op jit(solution)/shard_map/ppermute | solution.py:22
  64.5 7.9 %collective-permute-start.6 = (bf16[16,64,128]{2,1,0:T(8,128)(2,1)S(1)}, bf16[16,64,128]{2,1,0:T(8,128)(2,1)S(1)}, u32[]{:S(2)}, u32[]{:S(2)}) collective-permute-start(bf16[16,64,128]{2,1,0:T(8,128)(2,1)S(1)} %fusion.22), channel_id=1, source_target_pairs={{0,4},{4,0},{8,12},{12,8},{16,20},{20,16},{24,28},{28,24},{32,36},... | collective-permute-start | bytes 786440 | tf_op jit(solution)/shard_map/ppermute | solution.py:109
  72.4 0.8 copy-start.4
  72.4 0.8 copy-start.9
  76.8 2.2 %copy-start.1 = (bf16[256,2048]{1,0:T(8,128)(2,1)S(1)}, bf16[256,2048]{1,0:T(8,128)(2,1)}, u32[]{:S(2)}) copy-start(bf16[256,2048]{1,0:T(8,128)(2,1)} %param.13) | copy-start | bytes 3145732
Sparse Core Ops, SparseCore 0:
  10.1 105.2 all-gather.1
  133.6 29.6 reduce-scatter.1
